TPU v7x, 32 devices: a whole 2x2x4 slice. The times are simulated.
32 devices in a mesh: lat: 4 (over y, x), lon: 8 (over z, core).
Axes of the slice: x: 2, y: 2, z: 4, core: 2. Of those that a mesh axis runs over, the one named last changes fastest.
Arguments:
- right_side: float32 [512, 2048], P('lat', 'lon'), may hold values from -12 to 12
- diagonal: float32 [512, 2048], P('lat', 'lon'), may hold values from 0.2 to 2
- east_coef: float32 [512, 2048], P('lat', 'lon'), may hold values from 0.5 to 2
- north_coef: float32 [512, 2048], P('lat', 'lon'), may hold values from 0.5 to 2
- land_sea: int32 [512, 2048], P('lat', 'lon'), may hold values 0 or 1
- fold_partner: int32 [2048], P('lon'), may hold values from 0 to 2047, as said below
Outputs:
- solution_field: float32 [512, 2048], P('lat', 'lon')
- residual: float32 [512, 2048], P('lat', 'lon')
Inputs may be any that keep to these rules, and one draw needn't show every extreme that they name: fold_partner[fold_partner[i]] = i and fold_partner[i] != i for every column i, and fold_partner[i] // 256 = 7 - i // 256.
All inputs are finite; a program needn't handle non-finite values. No bound on the sum of `land_sea` on one device may be relied on, other than what follows from the above.
Results may differ from a plain program's by a relative error of at most 0.00019.
Values sent between devices are 32-bit elements; how exact they have to be, the bound alone decides.
A program may use at most 64 MiB of HBM per device.

v0:
```python
import jax
import jax.numpy as jnp
from jax import lax
from jax.sharding import PartitionSpec as P

ITERS = 4


def with_halo(cells, sides, width, closed):
    for axis, dim in sides:
        count = lax.axis_size(axis)
        ends = count if closed else count - 1
        head = lax.slice_in_dim(cells, 0, width, axis=dim)
        tail = lax.slice_in_dim(cells, cells.shape[dim] - width, cells.shape[dim], axis=dim)
        cells = jnp.concatenate(
            [
                lax.ppermute(tail, axis, [(i, (i + 1) % count) for i in range(ends)]),
                cells,
                lax.ppermute(head, axis, [((i + 1) % count, i) for i in range(ends)]),
            ],
            axis=dim,
        )
    return cells


def zonal_rim(values):
    return with_halo(values, (("lon", 1),), 1, True)


def meridional_rim(values):
    return with_halo(values, (("lat", 0),), 1, False)


def paired(residual, image):
    return lax.psum((jnp.sum(residual * residual), jnp.sum(residual * image)), ("lat", "lon"))


def local(right_side, diagonal, east_coef, north_coef, land_sea, fold_partner):
    row_count, col_count = right_side.shape
    ocean = land_sea.astype(jnp.float32)
    on_top = lax.axis_index("lat") == lax.axis_size("lat") - 1
    row_ids = lax.broadcasted_iota(jnp.int32, (row_count, col_count), 0)
    north_inner = jnp.where(on_top & (row_ids == row_count - 1), 0.0, north_coef)
    west_coef = zonal_rim(east_coef)[:, :col_count]
    south_coef = meridional_rim(north_inner)[:row_count]

    def neighbours(masked):
        across_lon = zonal_rim(masked)
        across_lat = meridional_rim(masked)
        return (
            across_lon[:, 2:],
            across_lon[:, :col_count],
            across_lat[2:],
            across_lat[:row_count],
        )

    def mirror_row(top_values):
        whole_row = lax.all_gather(top_values, "lon", axis=0, tiled=True)
        return jnp.take(whole_row, fold_partner, axis=0)

    top_coef = north_coef[row_count - 1]
    fold_coef = jnp.where(on_top, 0.5 * (top_coef + mirror_row(top_coef)), 0.0)

    def operate(surface):
        masked = ocean * surface
        east_vals, west_vals, north_vals, south_vals = neighbours(masked)
        spread = east_coef * (masked - east_vals) + west_coef * (masked - west_vals)
        spread = spread + north_inner * (masked - north_vals) + south_coef * (masked - south_vals)
        last_row = masked[row_count - 1]
        spread = spread.at[row_count - 1].add(fold_coef * (last_row - mirror_row(last_row)))
        return diagonal * surface + ocean * spread

    solution_field = jnp.zeros_like(right_side)
    residual = right_side
    image = operate(residual)
    norm_now, product = paired(residual, image)
    alpha = norm_now / product
    direction, along = (residual, image)
    for iteration in range(ITERS):
        solution_field = solution_field + alpha * direction
        residual = residual - alpha * along
        if iteration + 1 < ITERS:
            image = operate(residual)
            norm_next, product = paired(residual, image)
            ratio = norm_next / norm_now
            alpha = norm_next / (product - ratio * norm_next / alpha)
            direction = residual + ratio * direction
            along = image + ratio * along
            norm_now = norm_next
    return (solution_field, residual)


def solution(mesh):
    placed = (
        P("lat", "lon"),
        P("lat", "lon"),
        P("lat", "lon"),
        P("lat", "lon"),
        P("lat", "lon"),
        P("lon"),
    )
    return jax.shard_map(
        local,
        mesh=mesh,
        in_specs=placed,
        out_specs=(P("lat", "lon"), P("lat", "lon")),
        check_vma=False,
    )
```

profile of v0, /device:TPU:12, one launch (start us, length us, event | category | flops | bytes accessed | tf_op | source)
XLA Modules:
  0.0 291.9 jit_solution(6611212178361798222)
XLA Ops:
  1.8 3.4 %collective-permute-start.4 = (f32[1,256]{1,0:T(1,128)S(1)}, f32[1,256]{1,0:T(1,128)S(1)}, u32[]{:S(2)}, u32[]{:S(2)}) collective-permute-start(f32[1,256]{1,0:T(1,128)S(1)} %slice.255), channel_id=1, source_target_pairs={{0,8},{8,16},{16,24},{1,9},{9,17},{17,25},{2,10},{10,18},{18,26},{... | collective-permute-start | bytes 3080 | tf_op jit(solution)/shard_map/ppermute | solution.py:17
  5.3 3.3 %collective-permute-start.3 = (f32[1,256]{1,0:T(1,128)S(1)}, f32[1,256]{1,0:T(1,128)S(1)}, u32[]{:S(2)}, u32[]{:S(2)}) collective-permute-start(f32[1,256]{1,0:T(1,128)S(1)} %get-tuple-element.87), channel_id=1, source_target_pairs={{8,0},{16,8},{24,16},{9,1},{17,9},{25,17},{10,2},{18,10},{26,18},{... | collective-permute-start | bytes 3080 | tf_op jit(solution)/shard_map/ppermute | solution.py:19
  8.6 2.5 collective-permute-start.5
  12.1 10.8 %all-gather.1 = f32[1,2048]{1,0:T(1,128)S(1)} all-gather(f32[1,256]{1,0:T(1,128)S(1)} %get-tuple-element.88), channel_id=3, replica_groups=mesh['lat'=4,'lon'=8] {'lon'}, dimensions={1}, use_global_device_ids=true | all-gather | bytes 9216 | tf_op jit(solution)/shard_map/all_gather | solution.py:58
  22.9 10.2 %all-gather = f32[1,2048]{1,0:T(1,128)S(1)} all-gather(f32[1,256]{1,0:T(1,128)S(1)} %slice.214), channel_id=2, replica_groups=mesh['lat'=4,'lon'=8] {'lon'}, dimensions={1}, use_global_device_ids=true | all-gather | bytes 9216 | tf_op jit(solution)/shard_map/all_gather | solution.py:58
  33.1 1.7 gather_fusion
  34.8 1.7 gather_fusion.1
  37.0 3.3 %collective-permute-done.2 = f32[128,1]{1,0:T(8,128)S(1)} collective-permute-done((f32[128,1]{1,0:T(8,128)S(1)}, f32[128,1]{1,0:T(8,128)S(1)}, u32[]{:S(2)}, u32[]{:S(2)}) %collective-permute-start.2) | collective-permute-done | bytes 544 | tf_op jit(solution)/shard_map/ppermute | solution.py:17
  41.3 41.4 %all-reduce.3 = (f32[]{:T(128)}, f32[]{:T(128)}) all-reduce(f32[]{:T(128)} %get-tuple-element.58, f32[]{:T(128)} %get-tuple-element.57), channel_id=1, replica_groups=mesh['lat'=4,'lon'=8] {'lat','lon'}, use_global_device_ids=true, to_apply=%region_1.2 | all-reduce | flops 2 | bytes 16 | tf_op jit(solution)/shard_map/psum | solution.py:35
  84.1 8.3 %all-gather.2 = f32[1,2048]{1,0:T(1,128)S(1)} all-gather(f32[1,256]{1,0:T(1,128)S(1)} %get-tuple-element.84), channel_id=4, replica_groups=mesh['lat'=4,'lon'=8] {'lon'}, dimensions={1}, use_global_device_ids=true | all-gather | bytes 9216 | tf_op jit(solution)/shard_map/all_gather | solution.py:58
  92.4 3.8 %collective-permute-start.9 = (f32[1,256]{1,0:T(1,128)S(1)}, f32[1,256]{1,0:T(1,128)S(1)}, u32[]{:S(2)}, u32[]{:S(2)}) collective-permute-start(f32[1,256]{1,0:T(1,128)S(1)} %get-tuple-element.84), channel_id=1, source_target_pairs={{0,8},{8,16},{16,24},{1,9},{9,17},{17,25},{2,10},{10,18},{18,26},{... | collective-permute-start | bytes 3080 | tf_op jit(solution)/shard_map/ppermute | solution.py:17
  96.3 1.7 gather_fusion.2
  98.1 2.9 collective-permute-start.8
  102.5 1.9 collective-permute-done.6
  104.4 1.8 collective-permute-done.7
  107.2 42.0 %all-reduce.2 = (f32[]{:T(128)}, f32[]{:T(128)}) all-reduce(f32[]{:T(128)} %get-tuple-element.54, f32[]{:T(128)} %get-tuple-element.53), channel_id=1, replica_groups=mesh['lat'=4,'lon'=8] {'lat','lon'}, use_global_device_ids=true, to_apply=%region_5.7 | all-reduce | flops 2 | bytes 16 | tf_op jit(solution)/shard_map/psum | solution.py:35
  153.9 8.1 %all-gather.3 = f32[1,2048]{1,0:T(1,128)S(1)} all-gather(f32[1,256]{1,0:T(1,128)S(1)} %get-tuple-element.80), channel_id=5, replica_groups=mesh['lat'=4,'lon'=8] {'lon'}, dimensions={1}, use_global_device_ids=true | all-gather | bytes 9216 | tf_op jit(solution)/shard_map/all_gather | solution.py:58
  162.0 2.8 collective-permute-start.13
  164.9 1.7 gather_fusion.3
  166.6 3.9 %collective-permute-start.12 = (f32[1,256]{1,0:T(1,128)S(1)}, f32[1,256]{1,0:T(1,128)S(1)}, u32[]{:S(2)}, u32[]{:S(2)}) collective-permute-start(f32[1,256]{1,0:T(1,128)S(1)} %get-tuple-element.79), channel_id=1, source_target_pairs={{8,0},{16,8},{24,16},{9,1},{17,9},{25,17},{10,2},{18,10},{26,18},{... | collective-permute-start | bytes 3080 | tf_op jit(solution)/shard_map/ppermute | solution.py:19
  170.6 1.7 collective-permute-start.10
  172.3 1.9 collective-permute-done.10
  174.2 1.8 collective-permute-done.11
  177.0 40.9 %all-reduce.1 = (f32[]{:T(128)}, f32[]{:T(128)}) all-reduce(f32[]{:T(128)} %get-tuple-element.52, f32[]{:T(128)} %get-tuple-element.51), channel_id=1, replica_groups=mesh['lat'=4,'lon'=8] {'lat','lon'}, use_global_device_ids=true, to_apply=%region_9.11 | all-reduce | flops 2 | bytes 16 | tf_op jit(solution)/shard_map/psum | solution.py:35
  221.9 8.2 %all-gather.4 = f32[1,2048]{1,0:T(1,128)S(1)} all-gather(f32[1,256]{1,0:T(1,128)S(1)} %get-tuple-element.76), channel_id=6, replica_groups=mesh['lat'=4,'lon'=8] {'lon'}, dimensions={1}, use_global_device_ids=true | all-gather | bytes 9216 | tf_op jit(solution)/shard_map/all_gather | solution.py:58
  230.1 3.8 %collective-permute-start.17 = (f32[1,256]{1,0:T(1,128)S(1)}, f32[1,256]{1,0:T(1,128)S(1)}, u32[]{:S(2)}, u32[]{:S(2)}) collective-permute-start(f32[1,256]{1,0:T(1,128)S(1)} %get-tuple-element.76), channel_id=1, source_target_pairs={{0,8},{8,16},{16,24},{1,9},{9,17},{17,25},{2,10},{10,18},{18,26},{... | collective-permute-start | bytes 3080 | tf_op jit(solution)/shard_map/ppermute | solution.py:17
  234.0 1.7 gather_fusion.4
  235.7 2.9 collective-permute-start.16
  238.6 1.7 collective-permute-start.14
  240.3 1.9 collective-permute-done.14
  242.2 1.8 collective-permute-done.15
  244.9 42.0 %all-reduce = (f32[]{:T(128)}, f32[]{:T(128)}) all-reduce(f32[]{:T(128)} %get-tuple-element.56, f32[]{:T(128)} %get-tuple-element.55), channel_id=1, replica_groups=mesh['lat'=4,'lon'=8] {'lat','lon'}, use_global_device_ids=true, to_apply=%region_13.15 | all-reduce | flops 2 | bytes 16 | tf_op jit(solution)/shard_map/psum | solution.py:35
  (70 shorter events, 9.2 us)
Async XLA Ops:
  0.6 1.0 copy-start.4
  1.6 35.0 %collective-permute-start.1 = (f32[128,1]{1,0:T(8,128)S(1)}, f32[128,1]{1,0:T(8,128)S(1)}, u32[]{:S(2)}, u32[]{:S(2)}) collective-permute-start(f32[128,1]{1,0:T(8,128)S(1)} %slice.203), channel_id=1, source_target_pairs={{0,1},{1,2},{2,3},{3,4},{4,5},{5,6},{6,7},{7,0},{8,9},{9,10},{10,1... | collective-permute-start | bytes 1544 | tf_op jit(solution)/shard_map/ppermute | solution.py:17
  1.7 3.5 %copy-start = (s32[128,256]{1,0:T(8,128)S(1)}, s32[128,256]{1,0:T(8,128)}, u32[]{:S(2)}) copy-start(s32[128,256]{1,0:T(8,128)} %param.20) | copy-start | bytes 393220
  1.7 3.5 %copy-start.1 = (f32[128,256]{1,0:T(8,128)S(1)}, f32[128,256]{1,0:T(8,128)}, u32[]{:S(2)}) copy-start(f32[128,256]{1,0:T(8,128)} %param.16) | copy-start | bytes 393220
  1.8 38.5 %collective-permute-start.4 = (f32[1,256]{1,0:T(1,128)S(1)}, f32[1,256]{1,0:T(1,128)S(1)}, u32[]{:S(2)}, u32[]{:S(2)}) collective-permute-start(f32[1,256]{1,0:T(1,128)S(1)} %slice.255), channel_id=1, source_target_pairs={{0,8},{8,16},{16,24},{1,9},{9,17},{17,25},{2,10},{10,18},{18,26},{... | collective-permute-start | bytes 3080 | tf_op jit(solution)/shard_map/ppermute | solution.py:17
  5.3 35.0 %collective-permute-start.3 = (f32[1,256]{1,0:T(1,128)S(1)}, f32[1,256]{1,0:T(1,128)S(1)}, u32[]{:S(2)}, u32[]{:S(2)}) collective-permute-start(f32[1,256]{1,0:T(1,128)S(1)} %get-tuple-element.87), channel_id=1, source_target_pairs={{8,0},{16,8},{24,16},{9,1},{17,9},{25,17},{10,2},{18,10},{26,18},{... | collective-permute-start | bytes 3080 | tf_op jit(solution)/shard_map/ppermute | solution.py:19
  8.6 31.7 %collective-permute-start.5 = (f32[1,256]{1,0:T(1,128)S(1)}, f32[1,256]{1,0:T(1,128)S(1)}, u32[]{:S(2)}, u32[]{:S(2)}) collective-permute-start(f32[1,256]{1,0:T(1,128)S(1)} %get-tuple-element.88), channel_id=1, source_target_pairs={{0,8},{8,16},{16,24},{1,9},{9,17},{17,25},{2,10},{10,18},{18,26},{... | collective-permute-start | bytes 3080 | tf_op jit(solution)/shard_map/ppermute | solution.py:17
  11.2 25.8 %collective-permute-start = (f32[128,1]{1,0:T(8,128)S(1)}, f32[128,1]{1,0:T(8,128)S(1)}, u32[]{:S(2)}, u32[]{:S(2)}) collective-permute-start(f32[128,1]{1,0:T(8,128)S(1)} %get-tuple-element.85), channel_id=1, source_target_pairs={{1,0},{2,1},{3,2},{4,3},{5,4},{6,5},{7,6},{0,7},{9,8},{10,9},{11,1... | collective-permute-start | bytes 1544 | tf_op jit(solution)/shard_map/ppermute | solution.py:19
  12.1 10.8 %copy-start.5 = (s32[256]{0:T(256)S(1)}, s32[256]{0:T(256)}, u32[]{:S(2)}) copy-start(s32[256]{0:T(256)} %param.21) | copy-start | bytes 3076
  34.8 5.5 %copy-start.3 = (f32[128,256]{1,0:T(8,128)S(1)}, f32[128,256]{1,0:T(8,128)}, u32[]{:S(2)}) copy-start(f32[128,256]{1,0:T(8,128)} %param.18) | copy-start | bytes 393220
  36.6 3.7 %collective-permute-start.2 = (f32[128,1]{1,0:T(8,128)S(1)}, f32[128,1]{1,0:T(8,128)S(1)}, u32[]{:S(2)}, u32[]{:S(2)}) collective-permute-start(f32[128,1]{1,0:T(8,128)S(1)} %get-tuple-element.86), channel_id=1, source_target_pairs={{0,1},{1,2},{2,3},{3,4},{4,5},{5,6},{6,7},{7,0},{8,9},{9,10},{10,1... | collective-permute-start | bytes 1544 | tf_op jit(solution)/shard_map/ppermute | solution.py:17
  37.0 3.6 %copy-start.2 = (f32[128,256]{1,0:T(8,128)S(1)}, f32[128,256]{1,0:T(8,128)}, u32[]{:S(2)}) copy-start(f32[128,256]{1,0:T(8,128)} %param.17) | copy-start | bytes 393220
  92.4 13.8 %collective-permute-start.9 = (f32[1,256]{1,0:T(1,128)S(1)}, f32[1,256]{1,0:T(1,128)S(1)}, u32[]{:S(2)}, u32[]{:S(2)}) collective-permute-start(f32[1,256]{1,0:T(1,128)S(1)} %get-tuple-element.84), channel_id=1, source_target_pairs={{0,8},{8,16},{16,24},{1,9},{9,17},{17,25},{2,10},{10,18},{18,26},{... | collective-permute-start | bytes 3080 | tf_op jit(solution)/shard_map/ppermute | solution.py:17
  98.1 8.1 %collective-permute-start.8 = (f32[1,256]{1,0:T(1,128)S(1)}, f32[1,256]{1,0:T(1,128)S(1)}, u32[]{:S(2)}, u32[]{:S(2)}) collective-permute-start(f32[1,256]{1,0:T(1,128)S(1)} %get-tuple-element.83), channel_id=1, source_target_pairs={{8,0},{16,8},{24,16},{9,1},{17,9},{25,17},{10,2},{18,10},{26,18},{... | collective-permute-start | bytes 3080 | tf_op jit(solution)/shard_map/ppermute | solution.py:19
  101.0 3.4 %collective-permute-start.6 = (f32[128,1]{1,0:T(8,128)S(1)}, f32[128,1]{1,0:T(8,128)S(1)}, u32[]{:S(2)}, u32[]{:S(2)}) collective-permute-start(f32[128,1]{1,0:T(8,128)S(1)} %get-tuple-element.81), channel_id=1, source_target_pairs={{1,0},{2,1},{3,2},{4,3},{5,4},{6,5},{7,6},{0,7},{9,8},{10,9},{11,1... | collective-permute-start | bytes 1544 | tf_op jit(solution)/shard_map/ppermute | solution.py:19
  102.5 3.7 %collective-permute-start.7 = (f32[128,1]{1,0:T(8,128)S(1)}, f32[128,1]{1,0:T(8,128)S(1)}, u32[]{:S(2)}, u32[]{:S(2)}) collective-permute-start(f32[128,1]{1,0:T(8,128)S(1)} %get-tuple-element.82), channel_id=1, source_target_pairs={{0,1},{1,2},{2,3},{3,4},{4,5},{5,6},{6,7},{7,0},{8,9},{9,10},{10,1... | collective-permute-start | bytes 1544 | tf_op jit(solution)/shard_map/ppermute | solution.py:17
  162.0 14.0 %collective-permute-start.13 = (f32[1,256]{1,0:T(1,128)S(1)}, f32[1,256]{1,0:T(1,128)S(1)}, u32[]{:S(2)}, u32[]{:S(2)}) collective-permute-start(f32[1,256]{1,0:T(1,128)S(1)} %get-tuple-element.80), channel_id=1, source_target_pairs={{0,8},{8,16},{16,24},{1,9},{9,17},{17,25},{2,10},{10,18},{18,26},{... | collective-permute-start | bytes 3080 | tf_op jit(solution)/shard_map/ppermute | solution.py:17
  166.6 9.4 %collective-permute-start.12 = (f32[1,256]{1,0:T(1,128)S(1)}, f32[1,256]{1,0:T(1,128)S(1)}, u32[]{:S(2)}, u32[]{:S(2)}) collective-permute-start(f32[1,256]{1,0:T(1,128)S(1)} %get-tuple-element.79), channel_id=1, source_target_pairs={{8,0},{16,8},{24,16},{9,1},{17,9},{25,17},{10,2},{18,10},{26,18},{... | collective-permute-start | bytes 3080 | tf_op jit(solution)/shard_map/ppermute | solution.py:19
  170.6 3.6 %collective-permute-start.10 = (f32[128,1]{1,0:T(8,128)S(1)}, f32[128,1]{1,0:T(8,128)S(1)}, u32[]{:S(2)}, u32[]{:S(2)}) collective-permute-start(f32[128,1]{1,0:T(8,128)S(1)} %get-tuple-element.77), channel_id=1, source_target_pairs={{1,0},{2,1},{3,2},{4,3},{5,4},{6,5},{7,6},{0,7},{9,8},{10,9},{11,1... | collective-permute-start | bytes 1544 | tf_op jit(solution)/shard_map/ppermute | solution.py:19
  172.3 3.7 %collective-permute-start.11 = (f32[128,1]{1,0:T(8,128)S(1)}, f32[128,1]{1,0:T(8,128)S(1)}, u32[]{:S(2)}, u32[]{:S(2)}) collective-permute-start(f32[128,1]{1,0:T(8,128)S(1)} %get-tuple-element.78), channel_id=1, source_target_pairs={{0,1},{1,2},{2,3},{3,4},{4,5},{5,6},{6,7},{7,0},{8,9},{9,10},{10,1... | collective-permute-start | bytes 1544 | tf_op jit(solution)/shard_map/ppermute | solution.py:17
  230.1 13.9 %collective-permute-start.17 = (f32[1,256]{1,0:T(1,128)S(1)}, f32[1,256]{1,0:T(1,128)S(1)}, u32[]{:S(2)}, u32[]{:S(2)}) collective-permute-start(f32[1,256]{1,0:T(1,128)S(1)} %get-tuple-element.76), channel_id=1, source_target_pairs={{0,8},{8,16},{16,24},{1,9},{9,17},{17,25},{2,10},{10,18},{18,26},{... | collective-permute-start | bytes 3080 | tf_op jit(solution)/shard_map/ppermute | solution.py:17
  235.7 8.3 %collective-permute-start.16 = (f32[1,256]{1,0:T(1,128)S(1)}, f32[1,256]{1,0:T(1,128)S(1)}, u32[]{:S(2)}, u32[]{:S(2)}) collective-permute-start(f32[1,256]{1,0:T(1,128)S(1)} %get-tuple-element.75), channel_id=1, source_target_pairs={{8,0},{16,8},{24,16},{9,1},{17,9},{25,17},{10,2},{18,10},{26,18},{... | collective-permute-start | bytes 3080 | tf_op jit(solution)/shard_map/ppermute | solution.py:19
  238.6 3.6 %collective-permute-start.14 = (f32[128,1]{1,0:T(8,128)S(1)}, f32[128,1]{1,0:T(8,128)S(1)}, u32[]{:S(2)}, u32[]{:S(2)}) collective-permute-start(f32[128,1]{1,0:T(8,128)S(1)} %get-tuple-element.73), channel_id=1, source_target_pairs={{1,0},{2,1},{3,2},{4,3},{5,4},{6,5},{7,6},{0,7},{9,8},{10,9},{11,1... | collective-permute-start | bytes 1544 | tf_op jit(solution)/shard_map/ppermute | solution.py:19
  240.3 3.7 %collective-permute-start.15 = (f32[128,1]{1,0:T(8,128)S(1)}, f32[128,1]{1,0:T(8,128)S(1)}, u32[]{:S(2)}, u32[]{:S(2)}) collective-permute-start(f32[128,1]{1,0:T(8,128)S(1)} %get-tuple-element.74), channel_id=1, source_target_pairs={{0,1},{1,2},{2,3},{3,4},{4,5},{5,6},{6,7},{7,0},{8,9},{9,10},{10,1... | collective-permute-start | bytes 1544 | tf_op jit(solution)/shard_map/ppermute | solution.py:17
where the time goes:
time: 293 us; the launch traced here: 292 us
  blocking collectives  212 us (72%)
  starting transfers between devices  35.7 us (12%)
  between operations  14.9 us (5%)
  waiting for transfers between devices  14.4 us (5%)
  local copies, waits for them, and re-layouts  10.1 us (3%)
  other arithmetic  4.81 us (2%)
    psum x4, blocking collectives, paired(): lax.psum((jnp.sum(residual * residual), jnp.sum(residual * image)), ('lat...  166 us
    all_gather x5, blocking collectives, mirror_row(): whole_row = lax.all_gather(top_values, 'lon', axis=0, tiled=True)  45.7 us
    ppermute x8, starting transfers between devices, with_halo(): lax.ppermute(head, axis, [((i + 1) % count, i) for i in range(ends)])  18.9 us
    ppermute x10, starting transfers between devices, with_halo(): lax.ppermute(tail, axis, [(i, (i + 1) % count) for i in range(ends)])  16.8 us
    ppermute x10, waiting for transfers between devices, with_halo(): lax.ppermute(tail, axis, [(i, (i + 1) % count) for i in range(ends)])  8.69 us
    gather x5, local copies, waits for them, and re-layouts, mirror_row(): return jnp.take(whole_row, fold_partner, axis=0)  8.62 us
  transfers between devices with their start and end apart: 18, of which 7 were waited for; matrix products, arithmetic and copies ran while one was open for 3% of the time, Pallas kernels for 0%

commit v1 on v0

--- a/solution.py
+++ b/solution.py
@@ -55,7 +55,9 @@
         )
 
     def mirror_row(top_values):
-        whole_row = lax.all_gather(top_values, "lon", axis=0, tiled=True)
+        whole_row = jnp.concatenate(
+            lax.all_to_all(jnp.stack([top_values] * lax.axis_size("lon")), "lon", 0, 0), axis=0
+        )
         return jnp.take(whole_row, fold_partner, axis=0)
 
     top_coef = north_coef[row_count - 1]

time: 293 us -> 270 us (0.922)
  blocking collectives: 212 us -> 163 us
  starting transfers between devices: 35.7 us -> 56.6 us
  local copies, waits for them, and re-layouts: 10.1 us -> 13.8 us
    all_gather x5 -> x0, blocking collectives: 45.7 us -> none  [mirror_row(): whole_row = lax.all_gather(top_values, 'lon', axis=0, tiled=True)]
    all_to_all x0 -> x5, starting transfers between devices: none -> 26.7 us  [mirror_row(): lax.all_to_all(jnp.stack([top_values] * lax.axis_size('lon')), 'lon', 0, 0)]
    all_to_all x0 -> x5, waiting for transfers between devices: none -> 14 us  [mirror_row(): lax.all_to_all(jnp.stack([top_values] * lax.axis_size('lon')), 'lon', 0, 0)]
    ppermute x10, waiting for transfers between devices: 8.69 us -> 0.03 us  [with_halo(): lax.ppermute(tail, axis, [(i, (i + 1) % count) for i in range(ends)])]
    ppermute x8, waiting for transfers between devices: 5.69 us -> 0.02 us  [with_halo(): lax.ppermute(head, axis, [((i + 1) % count, i) for i in range(ends)])]
    ppermute x8, starting transfers between devices: 18.9 us -> 13.7 us  [with_halo(): lax.ppermute(head, axis, [((i + 1) % count, i) for i in range(ends)])]
    psum x4, blocking collectives: 166 us -> 163 us  [paired(): lax.psum((jnp.sum(residual * residual), jnp.sum(residual * image)), ('lat...]
    another operation x0 -> x5, local copies, waits for them, and re-layouts: none -> 3.02 us  [mirror_row(): jnp.stack([top_values] * lax.axis_size('lon'))]
  transfers between devices with their start and end apart: 18 -> 23, of which waited for: 7 -> 4; matrix products, arithmetic and copies ran while one was open for 3% -> 2% of each run, Pallas kernels for 0% -> 0%
where the time goes in v1:
time: 270 us; the launch traced here: 267 us
  blocking collectives  163 us (60%)
  starting transfers between devices  56.6 us (21%)
  between operations  15.1 us (6%)
  waiting for transfers between devices  14.1 us (5%)
  local copies, waits for them, and re-layouts  13.8 us (5%)
  other arithmetic  4.81 us (2%)
    psum x4, blocking collectives, paired(): lax.psum((jnp.sum(residual * residual), jnp.sum(residual * image)), ('lat...  163 us
    all_to_all x5, starting transfers between devices, mirror_row(): lax.all_to_all(jnp.stack([top_values] * lax.axis_size('lon')), 'lon', 0, 0)  26.7 us
    ppermute x10, starting transfers between devices, with_halo(): lax.ppermute(tail, axis, [(i, (i + 1) % count) for i in range(ends)])  16.2 us
    all_to_all x5, waiting for transfers between devices, mirror_row(): lax.all_to_all(jnp.stack([top_values] * lax.axis_size('lon')), 'lon', 0, 0)  14 us
    ppermute x8, starting transfers between devices, with_halo(): lax.ppermute(head, axis, [((i + 1) % count, i) for i in range(ends)])  13.7 us
    gather x5, local copies, waits for them, and re-layouts, mirror_row(): return jnp.take(whole_row, fold_partner, axis=0)  8.6 us
  transfers between devices with their start and end apart: 23, of which 4 were waited for; matrix products, arithmetic and copies ran while one was open for 2% of the time, Pallas kernels for 0%

profile of v1, /device:TPU:12, one launch (start us, length us, event | category | flops | bytes accessed | tf_op | source)
XLA Modules:
  0.0 267.5 jit_solution(13068125819222462051)
XLA Ops:
  0.6 0.8 slice.214
  2.0 5.3 %all-to-all-start = ((f32[8,1,256]{2,1,0:T(1,128)}), f32[8,1,256]{2,1,0:T(1,128)S(1)}, u32[]{:S(2)}, u32[]{:S(2)}) async-start(f32[8,1,256]{2,1,0:T(1,128)} %stack.15), calls=%async_computation | async-start | bytes 16384 | tf_op jit(solution)/shard_map/all_to_all | solution.py:59
  7.3 0.9 slice.203
  8.5 3.4 %collective-permute-start.4 = (f32[1,256]{1,0:T(1,128)S(1)}, f32[1,256]{1,0:T(1,128)S(1)}, u32[]{:S(2)}, u32[]{:S(2)}) collective-permute-start(f32[1,256]{1,0:T(1,128)S(1)} %slice.255), channel_id=1, source_target_pairs={{0,8},{8,16},{16,24},{1,9},{9,17},{17,25},{2,10},{10,18},{18,26},{... | collective-permute-start | bytes 3080 | tf_op jit(solution)/shard_map/ppermute | solution.py:17
  12.0 3.3 %collective-permute-start.3 = (f32[1,256]{1,0:T(1,128)S(1)}, f32[1,256]{1,0:T(1,128)S(1)}, u32[]{:S(2)}, u32[]{:S(2)}) collective-permute-start(f32[1,256]{1,0:T(1,128)S(1)} %get-tuple-element.87), channel_id=1, source_target_pairs={{8,0},{16,8},{24,16},{9,1},{17,9},{25,17},{10,2},{18,10},{26,18},{... | collective-permute-start | bytes 3080 | tf_op jit(solution)/shard_map/ppermute | solution.py:19
  15.4 2.6 collective-permute-start.5
  18.1 0.8 collective-permute-start
  20.0 6.2 %all-to-all-start.1 = ((f32[8,1,256]{2,1,0:T(1,128)}), f32[8,1,256]{2,1,0:T(1,128)S(1)}, u32[]{:S(2)}, u32[]{:S(2)}) async-start(f32[8,1,256]{2,1,0:T(1,128)} %stack.16), calls=%async_computation.1 | async-start | bytes 16384 | tf_op jit(solution)/shard_map/all_to_all | solution.py:59
  26.5 1.7 gather_fusion
  28.2 2.2 all-to-all-done.1
  30.4 1.7 gather_fusion.1
  32.9 40.7 %all-reduce.3 = (f32[]{:T(128)}, f32[]{:T(128)}) all-reduce(f32[]{:T(128)} %get-tuple-element.58, f32[]{:T(128)} %get-tuple-element.57), channel_id=1, replica_groups=mesh['lat'=4,'lon'=8] {'lat','lon'}, use_global_device_ids=true, to_apply=%region_1.2 | all-reduce | flops 2 | bytes 16 | tf_op jit(solution)/shard_map/psum | solution.py:35
  74.9 3.2 %collective-permute-start.8 = (f32[1,256]{1,0:T(1,128)S(1)}, f32[1,256]{1,0:T(1,128)S(1)}, u32[]{:S(2)}, u32[]{:S(2)}) collective-permute-start(f32[1,256]{1,0:T(1,128)S(1)} %get-tuple-element.83), channel_id=1, source_target_pairs={{8,0},{16,8},{24,16},{9,1},{17,9},{25,17},{10,2},{18,10},{26,18},{... | collective-permute-start | bytes 3080 | tf_op jit(solution)/shard_map/ppermute | solution.py:19
  78.1 2.7 collective-permute-start.9
  82.0 5.0 %all-to-all-start.2 = ((f32[8,1,256]{2,1,0:T(1,128)}), f32[8,1,256]{2,1,0:T(1,128)S(1)}, u32[]{:S(2)}, u32[]{:S(2)}) async-start(f32[8,1,256]{2,1,0:T(1,128)} %stack.17), calls=%async_computation.2 | async-start | bytes 16384 | tf_op jit(solution)/shard_map/all_to_all | solution.py:59
  87.3 3.9 %all-to-all-done.2 = f32[8,1,256]{2,1,0:T(1,128)S(1)} async-done(((f32[8,1,256]{2,1,0:T(1,128)}), f32[8,1,256]{2,1,0:T(1,128)S(1)}, u32[]{:S(2)}, u32[]{:S(2)}) %all-to-all-start.2) | async-done | bytes 8224 | tf_op jit(solution)/shard_map/all_to_all | solution.py:59
  91.2 1.7 gather_fusion.2
  93.0 0.8 multiply_reduce_fusion.4
  93.8 40.8 %all-reduce.2 = (f32[]{:T(128)}, f32[]{:T(128)}) all-reduce(f32[]{:T(128)} %get-tuple-element.54, f32[]{:T(128)} %get-tuple-element.53), channel_id=1, replica_groups=mesh['lat'=4,'lon'=8] {'lat','lon'}, use_global_device_ids=true, to_apply=%region_5.7 | all-reduce | flops 2 | bytes 16 | tf_op jit(solution)/shard_map/psum | solution.py:35
  139.3 3.1 %collective-permute-start.12 = (f32[1,256]{1,0:T(1,128)S(1)}, f32[1,256]{1,0:T(1,128)S(1)}, u32[]{:S(2)}, u32[]{:S(2)}) collective-permute-start(f32[1,256]{1,0:T(1,128)S(1)} %get-tuple-element.79), channel_id=1, source_target_pairs={{8,0},{16,8},{24,16},{9,1},{17,9},{25,17},{10,2},{18,10},{26,18},{... | collective-permute-start | bytes 3080 | tf_op jit(solution)/shard_map/ppermute | solution.py:19
  142.4 2.7 %collective-permute-start.13 = (f32[1,256]{1,0:T(1,128)S(1)}, f32[1,256]{1,0:T(1,128)S(1)}, u32[]{:S(2)}, u32[]{:S(2)}) collective-permute-start(f32[1,256]{1,0:T(1,128)S(1)} %get-tuple-element.80), channel_id=1, source_target_pairs={{0,8},{8,16},{16,24},{1,9},{9,17},{17,25},{2,10},{10,18},{18,26},{... | collective-permute-start | bytes 3080 | tf_op jit(solution)/shard_map/ppermute | solution.py:17
  146.4 5.0 %all-to-all-start.3 = ((f32[8,1,256]{2,1,0:T(1,128)}), f32[8,1,256]{2,1,0:T(1,128)S(1)}, u32[]{:S(2)}, u32[]{:S(2)}) async-start(f32[8,1,256]{2,1,0:T(1,128)} %stack.18), calls=%async_computation.3 | async-start | bytes 16384 | tf_op jit(solution)/shard_map/all_to_all | solution.py:59
  151.6 3.9 %all-to-all-done.3 = f32[8,1,256]{2,1,0:T(1,128)S(1)} async-done(((f32[8,1,256]{2,1,0:T(1,128)}), f32[8,1,256]{2,1,0:T(1,128)S(1)}, u32[]{:S(2)}, u32[]{:S(2)}) %all-to-all-start.3) | async-done | bytes 8224 | tf_op jit(solution)/shard_map/all_to_all | solution.py:59
  155.6 1.7 gather_fusion.3
  158.1 40.7 %all-reduce.1 = (f32[]{:T(128)}, f32[]{:T(128)}) all-reduce(f32[]{:T(128)} %get-tuple-element.52, f32[]{:T(128)} %get-tuple-element.51), channel_id=1, replica_groups=mesh['lat'=4,'lon'=8] {'lat','lon'}, use_global_device_ids=true, to_apply=%region_9.11 | all-reduce | flops 2 | bytes 16 | tf_op jit(solution)/shard_map/psum | solution.py:35
  203.0 3.2 %collective-permute-start.16 = (f32[1,256]{1,0:T(1,128)S(1)}, f32[1,256]{1,0:T(1,128)S(1)}, u32[]{:S(2)}, u32[]{:S(2)}) collective-permute-start(f32[1,256]{1,0:T(1,128)S(1)} %get-tuple-element.75), channel_id=1, source_target_pairs={{8,0},{16,8},{24,16},{9,1},{17,9},{25,17},{10,2},{18,10},{26,18},{... | collective-permute-start | bytes 3080 | tf_op jit(solution)/shard_map/ppermute | solution.py:19
  206.2 2.7 collective-permute-start.17
  210.1 5.0 %all-to-all-start.4 = ((f32[8,1,256]{2,1,0:T(1,128)}), f32[8,1,256]{2,1,0:T(1,128)S(1)}, u32[]{:S(2)}, u32[]{:S(2)}) async-start(f32[8,1,256]{2,1,0:T(1,128)} %stack.19), calls=%async_computation.4 | async-start | bytes 16384 | tf_op jit(solution)/shard_map/all_to_all | solution.py:59
  215.3 3.9 %all-to-all-done.4 = f32[8,1,256]{2,1,0:T(1,128)S(1)} async-done(((f32[8,1,256]{2,1,0:T(1,128)}), f32[8,1,256]{2,1,0:T(1,128)S(1)}, u32[]{:S(2)}, u32[]{:S(2)}) %all-to-all-start.4) | async-done | bytes 8224 | tf_op jit(solution)/shard_map/all_to_all | solution.py:59
  219.3 1.7 gather_fusion.4
  221.7 40.8 %all-reduce = (f32[]{:T(128)}, f32[]{:T(128)}) all-reduce(f32[]{:T(128)} %get-tuple-element.56, f32[]{:T(128)} %get-tuple-element.55), channel_id=1, replica_groups=mesh['lat'=4,'lon'=8] {'lat','lon'}, use_global_device_ids=true, to_apply=%region_13.15 | all-reduce | flops 2 | bytes 16 | tf_op jit(solution)/shard_map/psum | solution.py:35
  266.6 0.9 multiply_subtract_fusion
  (80 shorter events, 9.0 us)
Async XLA Ops:
  0.6 7.8 %copy-start.4 = (f32[128,256]{1,0:T(8,128)S(1)}, f32[128,256]{1,0:T(8,128)}, u32[]{:S(2)}) copy-start(f32[128,256]{1,0:T(8,128)} %param.19) | copy-start | bytes 393220
  2.0 17.4 %all-to-all-start = ((f32[8,1,256]{2,1,0:T(1,128)}), f32[8,1,256]{2,1,0:T(1,128)S(1)}, u32[]{:S(2)}, u32[]{:S(2)}) async-start(f32[8,1,256]{2,1,0:T(1,128)} %stack.15), calls=%async_computation | async-start | bytes 16384 | tf_op jit(solution)/shard_map/all_to_all | solution.py:59
  8.2 10.7 %collective-permute-start.1 = (f32[128,1]{1,0:T(8,128)S(1)}, f32[128,1]{1,0:T(8,128)S(1)}, u32[]{:S(2)}, u32[]{:S(2)}) collective-permute-start(f32[128,1]{1,0:T(8,128)S(1)} %slice.203), channel_id=1, source_target_pairs={{0,1},{1,2},{2,3},{3,4},{4,5},{5,6},{6,7},{7,0},{8,9},{9,10},{10,1... | collective-permute-start | bytes 1544 | tf_op jit(solution)/shard_map/ppermute | solution.py:17
  8.4 3.5 %copy-start = (s32[128,256]{1,0:T(8,128)S(1)}, s32[128,256]{1,0:T(8,128)}, u32[]{:S(2)}) copy-start(s32[128,256]{1,0:T(8,128)} %param.20) | copy-start | bytes 393220
  8.4 3.5 %copy-start.1 = (f32[128,256]{1,0:T(8,128)S(1)}, f32[128,256]{1,0:T(8,128)}, u32[]{:S(2)}) copy-start(f32[128,256]{1,0:T(8,128)} %param.16) | copy-start | bytes 393220
  8.5 17.7 %collective-permute-start.4 = (f32[1,256]{1,0:T(1,128)S(1)}, f32[1,256]{1,0:T(1,128)S(1)}, u32[]{:S(2)}, u32[]{:S(2)}) collective-permute-start(f32[1,256]{1,0:T(1,128)S(1)} %slice.255), channel_id=1, source_target_pairs={{0,8},{8,16},{16,24},{1,9},{9,17},{17,25},{2,10},{10,18},{18,26},{... | collective-permute-start | bytes 3080 | tf_op jit(solution)/shard_map/ppermute | solution.py:17
  12.0 14.3 %collective-permute-start.3 = (f32[1,256]{1,0:T(1,128)S(1)}, f32[1,256]{1,0:T(1,128)S(1)}, u32[]{:S(2)}, u32[]{:S(2)}) collective-permute-start(f32[1,256]{1,0:T(1,128)S(1)} %get-tuple-element.87), channel_id=1, source_target_pairs={{8,0},{16,8},{24,16},{9,1},{17,9},{25,17},{10,2},{18,10},{26,18},{... | collective-permute-start | bytes 3080 | tf_op jit(solution)/shard_map/ppermute | solution.py:19
  15.3 11.0 %copy-start.3 = (f32[128,256]{1,0:T(8,128)S(1)}, f32[128,256]{1,0:T(8,128)}, u32[]{:S(2)}) copy-start(f32[128,256]{1,0:T(8,128)} %param.18) | copy-start | bytes 393220
  15.4 10.9 %collective-permute-start.5 = (f32[1,256]{1,0:T(1,128)S(1)}, f32[1,256]{1,0:T(1,128)S(1)}, u32[]{:S(2)}, u32[]{:S(2)}) collective-permute-start(f32[1,256]{1,0:T(1,128)S(1)} %get-tuple-element.88), channel_id=1, source_target_pairs={{0,8},{8,16},{16,24},{1,9},{9,17},{17,25},{2,10},{10,18},{18,26},{... | collective-permute-start | bytes 3080 | tf_op jit(solution)/shard_map/ppermute | solution.py:17
  18.1 0.8 copy-start.5
  18.1 8.2 %collective-permute-start = (f32[128,1]{1,0:T(8,128)S(1)}, f32[128,1]{1,0:T(8,128)S(1)}, u32[]{:S(2)}, u32[]{:S(2)}) collective-permute-start(f32[128,1]{1,0:T(8,128)S(1)} %get-tuple-element.85), channel_id=1, source_target_pairs={{1,0},{2,1},{3,2},{4,3},{5,4},{6,5},{7,6},{0,7},{9,8},{10,9},{11,1... | collective-permute-start | bytes 1544 | tf_op jit(solution)/shard_map/ppermute | solution.py:19
  18.9 7.3 %collective-permute-start.2 = (f32[128,1]{1,0:T(8,128)S(1)}, f32[128,1]{1,0:T(8,128)S(1)}, u32[]{:S(2)}, u32[]{:S(2)}) collective-permute-start(f32[128,1]{1,0:T(8,128)S(1)} %get-tuple-element.86), channel_id=1, source_target_pairs={{0,1},{1,2},{2,3},{3,4},{4,5},{5,6},{6,7},{7,0},{8,9},{9,10},{10,1... | collective-permute-start | bytes 1544 | tf_op jit(solution)/shard_map/ppermute | solution.py:17
  20.0 10.4 %all-to-all-start.1 = ((f32[8,1,256]{2,1,0:T(1,128)}), f32[8,1,256]{2,1,0:T(1,128)S(1)}, u32[]{:S(2)}, u32[]{:S(2)}) async-start(f32[8,1,256]{2,1,0:T(1,128)} %stack.16), calls=%async_computation.1 | async-start | bytes 16384 | tf_op jit(solution)/shard_map/all_to_all | solution.py:59
  30.4 1.8 copy-start.2
  74.9 12.1 %collective-permute-start.8 = (f32[1,256]{1,0:T(1,128)S(1)}, f32[1,256]{1,0:T(1,128)S(1)}, u32[]{:S(2)}, u32[]{:S(2)}) collective-permute-start(f32[1,256]{1,0:T(1,128)S(1)} %get-tuple-element.83), channel_id=1, source_target_pairs={{8,0},{16,8},{24,16},{9,1},{17,9},{25,17},{10,2},{18,10},{26,18},{... | collective-permute-start | bytes 3080 | tf_op jit(solution)/shard_map/ppermute | solution.py:19
  78.1 8.9 %collective-permute-start.9 = (f32[1,256]{1,0:T(1,128)S(1)}, f32[1,256]{1,0:T(1,128)S(1)}, u32[]{:S(2)}, u32[]{:S(2)}) collective-permute-start(f32[1,256]{1,0:T(1,128)S(1)} %get-tuple-element.84), channel_id=1, source_target_pairs={{0,8},{8,16},{16,24},{1,9},{9,17},{17,25},{2,10},{10,18},{18,26},{... | collective-permute-start | bytes 3080 | tf_op jit(solution)/shard_map/ppermute | solution.py:17
  80.9 6.2 %collective-permute-start.6 = (f32[128,1]{1,0:T(8,128)S(1)}, f32[128,1]{1,0:T(8,128)S(1)}, u32[]{:S(2)}, u32[]{:S(2)}) collective-permute-start(f32[128,1]{1,0:T(8,128)S(1)} %get-tuple-element.81), channel_id=1, source_target_pairs={{1,0},{2,1},{3,2},{4,3},{5,4},{6,5},{7,6},{0,7},{9,8},{10,9},{11,1... | collective-permute-start | bytes 1544 | tf_op jit(solution)/shard_map/ppermute | solution.py:19
  80.9 6.1 %collective-permute-start.7 = (f32[128,1]{1,0:T(8,128)S(1)}, f32[128,1]{1,0:T(8,128)S(1)}, u32[]{:S(2)}, u32[]{:S(2)}) collective-permute-start(f32[128,1]{1,0:T(8,128)S(1)} %get-tuple-element.82), channel_id=1, source_target_pairs={{0,1},{1,2},{2,3},{3,4},{4,5},{5,6},{6,7},{7,0},{8,9},{9,10},{10,1... | collective-permute-start | bytes 1544 | tf_op jit(solution)/shard_map/ppermute | solution.py:17
  82.0 9.2 %all-to-all-start.2 = ((f32[8,1,256]{2,1,0:T(1,128)}), f32[8,1,256]{2,1,0:T(1,128)S(1)}, u32[]{:S(2)}, u32[]{:S(2)}) async-start(f32[8,1,256]{2,1,0:T(1,128)} %stack.17), calls=%async_computation.2 | async-start | bytes 16384 | tf_op jit(solution)/shard_map/all_to_all | solution.py:59
  139.3 12.1 %collective-permute-start.12 = (f32[1,256]{1,0:T(1,128)S(1)}, f32[1,256]{1,0:T(1,128)S(1)}, u32[]{:S(2)}, u32[]{:S(2)}) collective-permute-start(f32[1,256]{1,0:T(1,128)S(1)} %get-tuple-element.79), channel_id=1, source_target_pairs={{8,0},{16,8},{24,16},{9,1},{17,9},{25,17},{10,2},{18,10},{26,18},{... | collective-permute-start | bytes 3080 | tf_op jit(solution)/shard_map/ppermute | solution.py:19
  142.4 9.0 %collective-permute-start.13 = (f32[1,256]{1,0:T(1,128)S(1)}, f32[1,256]{1,0:T(1,128)S(1)}, u32[]{:S(2)}, u32[]{:S(2)}) collective-permute-start(f32[1,256]{1,0:T(1,128)S(1)} %get-tuple-element.80), channel_id=1, source_target_pairs={{0,8},{8,16},{16,24},{1,9},{9,17},{17,25},{2,10},{10,18},{18,26},{... | collective-permute-start | bytes 3080 | tf_op jit(solution)/shard_map/ppermute | solution.py:17
  145.2 6.2 %collective-permute-start.10 = (f32[128,1]{1,0:T(8,128)S(1)}, f32[128,1]{1,0:T(8,128)S(1)}, u32[]{:S(2)}, u32[]{:S(2)}) collective-permute-start(f32[128,1]{1,0:T(8,128)S(1)} %get-tuple-element.77), channel_id=1, source_target_pairs={{1,0},{2,1},{3,2},{4,3},{5,4},{6,5},{7,6},{0,7},{9,8},{10,9},{11,1... | collective-permute-start | bytes 1544 | tf_op jit(solution)/shard_map/ppermute | solution.py:19
  145.3 6.1 %collective-permute-start.11 = (f32[128,1]{1,0:T(8,128)S(1)}, f32[128,1]{1,0:T(8,128)S(1)}, u32[]{:S(2)}, u32[]{:S(2)}) collective-permute-start(f32[128,1]{1,0:T(8,128)S(1)} %get-tuple-element.78), channel_id=1, source_target_pairs={{0,1},{1,2},{2,3},{3,4},{4,5},{5,6},{6,7},{7,0},{8,9},{9,10},{10,1... | collective-permute-start | bytes 1544 | tf_op jit(solution)/shard_map/ppermute | solution.py:17
  146.4 9.2 %all-to-all-start.3 = ((f32[8,1,256]{2,1,0:T(1,128)}), f32[8,1,256]{2,1,0:T(1,128)S(1)}, u32[]{:S(2)}, u32[]{:S(2)}) async-start(f32[8,1,256]{2,1,0:T(1,128)} %stack.18), calls=%async_computation.3 | async-start | bytes 16384 | tf_op jit(solution)/shard_map/all_to_all | solution.py:59
  203.0 12.1 %collective-permute-start.16 = (f32[1,256]{1,0:T(1,128)S(1)}, f32[1,256]{1,0:T(1,128)S(1)}, u32[]{:S(2)}, u32[]{:S(2)}) collective-permute-start(f32[1,256]{1,0:T(1,128)S(1)} %get-tuple-element.75), channel_id=1, source_target_pairs={{8,0},{16,8},{24,16},{9,1},{17,9},{25,17},{10,2},{18,10},{26,18},{... | collective-permute-start | bytes 3080 | tf_op jit(solution)/shard_map/ppermute | solution.py:19
  206.2 8.9 %collective-permute-start.17 = (f32[1,256]{1,0:T(1,128)S(1)}, f32[1,256]{1,0:T(1,128)S(1)}, u32[]{:S(2)}, u32[]{:S(2)}) collective-permute-start(f32[1,256]{1,0:T(1,128)S(1)} %get-tuple-element.76), channel_id=1, source_target_pairs={{0,8},{8,16},{16,24},{1,9},{9,17},{17,25},{2,10},{10,18},{18,26},{... | collective-permute-start | bytes 3080 | tf_op jit(solution)/shard_map/ppermute | solution.py:17
  208.9 6.2 %collective-permute-start.14 = (f32[128,1]{1,0:T(8,128)S(1)}, f32[128,1]{1,0:T(8,128)S(1)}, u32[]{:S(2)}, u32[]{:S(2)}) collective-permute-start(f32[128,1]{1,0:T(8,128)S(1)} %get-tuple-element.73), channel_id=1, source_target_pairs={{1,0},{2,1},{3,2},{4,3},{5,4},{6,5},{7,6},{0,7},{9,8},{10,9},{11,1... | collective-permute-start | bytes 1544 | tf_op jit(solution)/shard_map/ppermute | solution.py:19
  209.0 6.1 %collective-permute-start.15 = (f32[128,1]{1,0:T(8,128)S(1)}, f32[128,1]{1,0:T(8,128)S(1)}, u32[]{:S(2)}, u32[]{:S(2)}) collective-permute-start(f32[128,1]{1,0:T(8,128)S(1)} %get-tuple-element.74), channel_id=1, source_target_pairs={{0,1},{1,2},{2,3},{3,4},{4,5},{5,6},{6,7},{7,0},{8,9},{9,10},{10,1... | collective-permute-start | bytes 1544 | tf_op jit(solution)/shard_map/ppermute | solution.py:17
  210.1 9.2 %all-to-all-start.4 = ((f32[8,1,256]{2,1,0:T(1,128)}), f32[8,1,256]{2,1,0:T(1,128)S(1)}, u32[]{:S(2)}, u32[]{:S(2)}) async-start(f32[8,1,256]{2,1,0:T(1,128)} %stack.19), calls=%async_computation.4 | async-start | bytes 16384 | tf_op jit(solution)/shard_map/all_to_all | solution.py:59
